TPU v7x, 32 devices: a whole 2x2x4 slice. The times are simulated.
32 devices in a mesh: expert: 8 (over z, y), replica: 4 (over x, core).
Axes of the slice: x: 2, y: 2, z: 4, core: 2. Of those that a mesh axis runs over, the one named last changes fastest.
Arguments:
- tokens: bfloat16 [2048, 2880], P(('expert', 'replica')), may hold values from -6 to 6
- expert_ids: int32 [2048, 4], P(('expert', 'replica')), may hold values from 0 to 7, all different within a row; in each aligned block of 64 rows (0 to 63, 64 to 127, ...) at most 48 rows name the same one
- gate_codes: int32 [2048, 4], P(('expert', 'replica')), may hold values from 1 to 65535
- w_gate: bfloat16 [8, 2880, 2880], P('expert', None, 'replica'), may hold values from -0.109375 to 0.109375
- w_up: bfloat16 [8, 2880, 2880], P('expert', None, 'replica'), may hold values from -0.109375 to 0.109375
- w_down: bfloat16 [8, 2880, 2880], P('expert', 'replica'), may hold values from -0.109375 to 0.109375
Outputs:
- mixed: bfloat16 [2048, 2880], P(('expert', 'replica'))
Inputs may be any that keep to these rules, and one draw needn't show every extreme that they name: `expert_ids`: each row names 4 different experts. Among the 64 rows of one device each expert is named at most 48 times, a bound that some block reaches.
All inputs are finite; a program needn't handle non-finite values.
Results may differ from a plain program's by a relative error of at most 0.015.
Values may be sent and summed in bfloat16 or wider, within the bound.
A program may use at most 128 MiB of HBM per device.

v0:
```python
import jax
import jax.numpy as jnp
from jax import lax
from jax.sharding import PartitionSpec as P


def activate(gate, up):
    return gate * jax.nn.sigmoid(1.702 * gate) * (up + 1.0)


def on_device(tokens, expert_ids, gate_codes, w_gate, w_up, w_down):
    tok_rows, top_count = expert_ids.shape
    width = tokens.shape[1]
    expert_count = lax.axis_size("expert") * w_gate.shape[0]
    capacity = 3 * tok_rows * top_count // (2 * expert_count)
    slot_count = expert_count * capacity
    flat_ids = expert_ids.reshape(-1)
    onehot = (flat_ids[:, None] == jnp.arange(expert_count, dtype=jnp.int32)[None, :]).astype(
        jnp.int32
    )
    ranking = jnp.sum((jnp.cumsum(onehot, axis=0) - 1) * onehot, axis=1)
    target = flat_ids * capacity + ranking
    picker = (target[:, None] == jnp.arange(slot_count, dtype=jnp.int32)[None, :]).astype(
        jnp.bfloat16
    )
    selector = jnp.sum(picker.reshape(tok_rows, top_count, slot_count), axis=1)
    outgoing = jnp.einsum("ts,td->sd", selector, tokens, preferred_element_type=jnp.float32).astype(
        jnp.bfloat16
    )
    arrived = lax.all_to_all(outgoing, "expert", split_axis=0, concat_axis=0, tiled=True)
    gathered = lax.all_gather(arrived, "replica", axis=0, tiled=True)
    gate = jnp.dot(gathered, w_gate[0], preferred_element_type=jnp.float32)
    up = jnp.dot(gathered, w_up[0], preferred_element_type=jnp.float32)
    hidden = activate(gate, up).astype(jnp.bfloat16)
    summed = lax.psum_scatter(
        jnp.dot(hidden, w_down[0], preferred_element_type=jnp.float32).astype(jnp.bfloat16),
        "replica",
        scatter_dimension=0,
        tiled=True,
    )
    returned = lax.all_to_all(summed, "expert", split_axis=0, concat_axis=0, tiled=True)
    per_choice = jnp.dot(picker, returned, preferred_element_type=jnp.float32)
    gates = gate_codes.astype(jnp.float32) / 65536.0
    weighted = per_choice.reshape(tok_rows, top_count, width) * gates[:, :, None]
    return jnp.sum(weighted, axis=1).astype(jnp.bfloat16)


def solution(mesh):
    return jax.shard_map(
        on_device,
        mesh=mesh,
        in_specs=(
            P(("expert", "replica"), None),
            P(("expert", "replica"), None),
            P(("expert", "replica"), None),
            P("expert", None, "replica"),
            P("expert", None, "replica"),
            P("expert", "replica", None),
        ),
        out_specs=P(("expert", "replica"), None),
        check_vma=False,
    )
```

profile of v0, /device:TPU:0, one launch (start us, length us, event | category | flops | bytes accessed | tf_op | source)
XLA Modules:
  0.0 323.3 jit_solution(10091895653846374134)
XLA Ops:
  6.5 0.0 copy-start
  6.5 0.0 all-gather.2.cloned.1.call-start
  6.5 0.8 copy.33
  7.4 0.1 eq.65
  7.5 0.1 eq.61
  7.6 0.6 reduce-window.6
  8.2 0.2 slice_reduce_fusion
  8.4 0.1 fusion.15
  8.5 0.1 reduce_sum.33
  8.6 0.1 copy.35
  8.7 0.7 multiply_add_fusion
  9.4 0.1 fusion.13
  9.5 0.0 copy-done
  9.5 0.8 convolution_convert_fusion.1
  10.3 2.6 copy.36
  12.9 59.4 %all_to_all.24 = bf16[8,48,2880]{2,1,0:T(8,128)(2,1)} all-to-all(bf16[8,48,2880]{2,1,0:T(8,128)(2,1)} %bitcast.35), channel_id=1, replica_groups=mesh['expert'=8,'replica'=4] {'expert'}, dimensions={0} | all-to-all | bytes 4423680 | tf_op jit(solution)/shard_map/all_to_all | solution.py:30
  72.3 0.0 all-gather.2.cloned.1.call-update
  72.3 0.0 reduce-scatter.4.cloned.1.call-start
  72.3 60.9 %all-gather.2.cloned.1.call-done = bf16[1536,2880]{1,0:T(8,128)(2,1)} async-done(((bf16[384,2880]{1,0:T(8,128)(2,1)}), bf16[1536,2880]{1,0:T(8,128)(2,1)}) %all-gather.2.cloned.1.call-update) | async-done | bytes 8847376 | tf_op jit(solution)/shard_map/all_gather | solution.py:31
  133.2 12.3 %fusion.1 = f32[1536,720]{0,1:T(8,128)} fusion(bf16[1536,2880]{1,0:T(8,128)(2,1)} %all-gather.2.cloned.1.call-done, bf16[1,2880,720]{1,2,0:T(8,128)(2,1)} %param.10), kind=kOutput, calls=%fused_computation.3 | convolution fusion | flops 6370099200 | bytes 17418240 | tf_op jit(solution)/shard_map/dot_general | solution.py:33
  145.6 23.8 %convolution_convert_fusion = bf16[1536,2880]{0,1:T(8,128)(2,1)} fusion(bf16[1,720,2880]{2,1,0:T(8,128)(2,1)} %param.11, f32[1536,720]{0,1:T(8,128)} %fusion.1, bf16[1536,2880]{1,0:T(8,128)(2,1)} %all-gather.2.cloned.1.call-done, bf16[1,2880,720]{1,2,0:T(8,128)(2,1)} %param.9), kind=kOutput, calls=%fused_computation | convolution fusion | flops 12753469440 | bytes 30412800 | tf_op jit(solution)/shard_map/dot_general | solution.py:36
  169.3 12.5 %copy.41 = bf16[1536,2880]{1,0:T(8,128)(2,1)} copy(bf16[1536,2880]{0,1:T(8,128)(2,1)} %convolution_convert_fusion) | data formatting | bytes 17694720
  181.8 0.0 reduce-scatter.4.cloned.1.call-update
  181.8 0.0 copy-start.1
  181.8 75.6 %reduce-scatter.4.cloned.1.call-done = bf16[384,2880]{1,0:T(8,128)(2,1)} async-done(((bf16[1536,2880]{1,0:T(8,128)(2,1)}), bf16[384,2880]{1,0:T(8,128)(2,1)}) %reduce-scatter.4.cloned.1.call-update) | async-done | bytes 2211856 | tf_op jit(solution)/shard_map/reduce_scatter | solution.py:35
  257.5 5.5 %all-to-all-start.1 = ((bf16[8,48,2880]{2,1,0:T(8,128)(2,1)}), bf16[8,48,2880]{2,1,0:T(8,128)(2,1)S(1)}, u32[]{:S(2)}, u32[]{:S(2)}) async-start(bf16[8,48,2880]{2,1,0:T(8,128)(2,1)} %bitcast.36), calls=%async_computation.1 | async-start | bytes 4521984 | tf_op jit(solution)/shard_map/all_to_all | solution.py:41
  263.0 0.0 copy-done.1
  263.0 51.6 %all-to-all-done.1 = bf16[8,48,2880]{2,1,0:T(8,128)(2,1)S(1)} async-done(((bf16[8,48,2880]{2,1,0:T(8,128)(2,1)}), bf16[8,48,2880]{2,1,0:T(8,128)(2,1)S(1)}, u32[]{:S(2)}, u32[]{:S(2)}) %all-to-all-start.1) | async-done | bytes 2211872 | tf_op jit(solution)/shard_map/all_to_all | solution.py:41
  314.6 1.8 fusion.9
  (4 shorter events, 0.1 us)
Async XLA Ops:
  6.5 3.0 copy-start
  6.5 126.7 %all-gather.2.cloned.1.call-start = ((), (), s32[]{:S(2)}) async-start(), calls=%async_computation.3 | async-start | bytes 11304960 | tf_op jit(solution)/shard_map/all_gather | solution.py:31
  72.3 185.2 %reduce-scatter.4.cloned.1.call-start = ((), (), s32[]{:S(2)}) async-start(), calls=%async_computation.4 | async-start | bytes 11304960 | tf_op jit(solution)/shard_map/reduce_scatter | solution.py:35
  181.8 81.2 %copy-start.1 = (s32[64,4]{0,1:T(4,128)S(1)}, s32[64,4]{0,1:T(4,128)}, u32[]{:S(2)}) copy-start(s32[64,4]{0,1:T(4,128)} %param.8) | copy-start | bytes 3076
  257.5 57.1 %all-to-all-start.1 = ((bf16[8,48,2880]{2,1,0:T(8,128)(2,1)}), bf16[8,48,2880]{2,1,0:T(8,128)(2,1)S(1)}, u32[]{:S(2)}, u32[]{:S(2)}) async-start(bf16[8,48,2880]{2,1,0:T(8,128)(2,1)} %bitcast.36), calls=%async_computation.1 | async-start | bytes 4521984 | tf_op jit(solution)/shard_map/all_to_all | solution.py:41
Sparse Core Ops, SparseCore 0:
  72.4 60.7 all-gather.1
  181.9 75.4 reduce-scatter.3
where the time goes:
time: 324 us; the launch traced here: 323 us
  waiting for transfers between devices  188 us (58%)
  blocking collectives  59.4 us (18%)
  matrix products  38.7 us (12%)
  local copies, waits for them, and re-layouts  16.5 us (5%)
  between operations  13.5 us (4%)
  starting transfers between devices  5.56 us (2%)
    reduce_scatter x1, waiting for transfers between devices, on_device(): lax.psum_scatter(jnp.dot(hidden, w_down[0], preferred_element_type=jnp.fl...  75.6 us
    all_gather x1, waiting for transfers between devices, on_device(): gathered = lax.all_gather(arrived, 'replica', axis=0, tiled=True)  60.9 us
    all_to_all x1, blocking collectives, on_device(): lax.all_to_all(outgoing, 'expert', split_axis=0, concat_axis=0, tiled=True)  59.4 us
    all_to_all x1, waiting for transfers between devices, on_device(): lax.all_to_all(summed, 'expert', split_axis=0, concat_axis=0, tiled=True)  51.6 us
    dot_general x1, matrix products, on_device(): jnp.dot(hidden, w_down[0], preferred_element_type=jnp.float32)  23.8 us
    unnamed x6, local copies, waits for them, and re-layouts  13.3 us
    dot_general x1, matrix products, on_device(): up = jnp.dot(gathered, w_up[0], preferred_element_type=jnp.float32)  12.3 us
  transfers between devices with their start and end apart: 3, of which 3 were waited for; matrix products, arithmetic and copies ran while one was open for 0% of the time, Pallas kernels for 0%

commit v1 on v0

--- a/solution.py
+++ b/solution.py
@@ -1,14 +1,245 @@
+import functools
+
 import jax
 import jax.numpy as jnp
 from jax import lax
+from jax.experimental import pallas as pl
+from jax.experimental.pallas import tpu as pltpu
 from jax.sharding import PartitionSpec as P
+
+MESH = pl.DeviceIdType.MESH
+CORES = 2
+LANES = 128
 
 
 def activate(gate, up):
     return gate * jax.nn.sigmoid(1.702 * gate) * (up + 1.0)
 
 
-def on_device(tokens, expert_ids, gate_codes, w_gate, w_up, w_down):
+def spans(extent, step):
+    return [(low, min(low + step, extent)) for low in range(0, extent, step)]
+
+
+def fused(
+    depth, experts, cap, tokens, meta, w_gate, w_up, w_down, out,
+    tok_buf, meta_buf, y_out, x_buf, wg, wu, wd, hid, part, c_in, x_out, x_in,
+    mine, y_in, z_out, z_in, acc, w_sem,
+    zt_s, zt_r, zm_s, zm_r, y_s, y_r, x_s, x_r, c_s, c_r,
+    pc_s, pc_r, px_s, px_r, py_s, py_r, pz_s, pz_r,
+):
+    rows, width = tokens.shape
+    f32, bf16 = jnp.float32, jnp.bfloat16
+    expert, replica = lax.axis_index("expert"), lax.axis_index("replica")
+    z, y = expert // 2, expert % 2
+    other = z * 2 + (1 - y)
+    y_peer = {"expert": other}
+    x_peer = {"replica": (replica + CORES) % (2 * CORES)}
+    c_peer = {"replica": replica // CORES * CORES + (1 - replica % CORES)}
+
+    def z_peer(back):
+        return {"expert": ((z + depth - back) % depth) * 2 + y}
+
+    def z_ahead(ahead):
+        return {"expert": ((z + ahead) % depth) * 2 + y}
+
+    def send(src, dst, ssem, rsem, peer):
+        pltpu.make_async_remote_copy(
+            src_ref=src, dst_ref=dst, send_sem=ssem, recv_sem=rsem,
+            device_id=peer, device_id_type=MESH,
+        ).start()
+
+    def arrived(dst, sem):
+        pltpu.make_async_copy(dst, dst, sem).wait()
+
+    barrier = pltpu.get_barrier_semaphore()
+    for peer in [z_peer(s) for s in range(1, depth)] + [y_peer, x_peer, c_peer]:
+        pl.semaphore_signal(barrier, inc=1, device_id=peer, device_id_type=MESH)
+    pl.semaphore_wait(barrier, depth + 2)
+
+    for s in range(1, depth):
+        send(meta, meta_buf.at[s], zm_s.at[s], zm_r.at[s], z_peer(s))
+        send(tokens, tok_buf.at[s], zt_s.at[s], zt_r.at[s], z_peer(s))
+    pltpu.make_async_copy(meta, meta_buf.at[0], zm_r.at[0]).start()
+    pltpu.make_async_copy(tokens, tok_buf.at[0], zt_r.at[0]).start()
+    loads = [
+        pltpu.make_async_copy(src.at[0], dst, w_sem.at[i])
+        for i, (src, dst) in enumerate(((w_gate, wg), (w_up, wu), (w_down, wd)))
+    ]
+    for load in loads:
+        load.start()
+
+    group = 2 * cap
+
+    def pick(s, which):
+        ranks = meta_buf[s, pl.ds(rows, 2 * experts), :]
+        sub = lax.broadcasted_iota(jnp.int32, ranks.shape, 0)
+        rank = jnp.sum(jnp.where(sub == which, ranks, 0.0), axis=0, keepdims=True)[:, :rows]
+        slot = lax.broadcasted_iota(jnp.int32, (cap, rows), 0).astype(f32)
+        return jnp.where(slot == rank, 1.0, 0.0).astype(bf16)
+
+    def spread(s, which):
+        ranks = meta_buf[s, pl.ds(0, rows), :]
+        lane = lax.broadcasted_iota(jnp.int32, ranks.shape, 1)
+        rank = jnp.sum(jnp.where(lane == which, ranks, 0.0), axis=1, keepdims=True)
+        weight = jnp.sum(jnp.where(lane == which + experts, ranks, 0.0), axis=1, keepdims=True)
+        slot = lax.broadcasted_iota(jnp.int32, (rows, cap), 1).astype(f32)
+        return jnp.where(slot == rank, 1.0, 0.0).astype(bf16), weight
+
+    def choose(s):
+        arrived(meta_buf.at[s], zm_r.at[s])
+        arrived(tok_buf.at[s], zt_r.at[s])
+        block = tok_buf[s]
+        y_out[s] = jnp.dot(pick(s, other), block, preferred_element_type=f32).astype(bf16)
+        send(y_out.at[s], x_buf.at[s, pl.ds(cap, cap)], y_s.at[s], y_r.at[s], y_peer)
+        x_buf[s, pl.ds(0, cap), :] = jnp.dot(
+            pick(s, expert), block, preferred_element_type=f32
+        ).astype(bf16)
+
+    def to_x(s):
+        arrived(y_out.at[s], y_r.at[s])
+        send(x_buf.at[s, pl.ds(0, group)], x_buf.at[s, pl.ds(group, group)],
+             x_s.at[s], x_r.at[s], x_peer)
+
+    def to_core(s):
+        arrived(x_in.at[s], x_r.at[s])
+        send(x_buf.at[s, pl.ds(0, 2 * group)], x_buf.at[s, pl.ds(2 * group, 2 * group)],
+             c_s.at[s], c_r.at[s], c_peer)
+
+    def ffn(s):
+        arrived(c_in.at[s], c_r.at[s])
+
+        @pl.when(s == 0)
+        def _():
+            for load in loads:
+                load.wait()
+
+        for low, high in spans(wg.shape[1], 256):
+            block = x_buf[s]
+            gate = jnp.dot(block, wg[:, low:high], preferred_element_type=f32)
+            up = jnp.dot(block, wu[:, low:high], preferred_element_type=f32)
+            hid[:, low:high] = activate(gate, up).astype(bf16)
+        for low, high in spans(width, 512):
+            part[s, :, low:high] = jnp.dot(
+                hid[...], wd[:, low:high], preferred_element_type=f32
+            ).astype(bf16)
+        send(part.at[s, pl.ds(2 * group, 2 * group)], c_in.at[s], pc_s.at[s], pc_r.at[s], c_peer)
+
+    def sum_core(s):
+        arrived(c_in.at[s], pc_r.at[s])
+        x_out[s] = (
+            part[s, pl.ds(group, group), :].astype(f32) + c_in[s, pl.ds(group, group), :].astype(f32)
+        ).astype(bf16)
+        send(x_out.at[s], x_in.at[s], px_s.at[s], px_r.at[s], x_peer)
+
+    def sum_x(s):
+        arrived(x_in.at[s], px_r.at[s])
+        mine[s] = (
+            part[s, pl.ds(0, group), :].astype(f32)
+            + c_in[s, pl.ds(0, group), :].astype(f32)
+            + x_in[s].astype(f32)
+        ).astype(bf16)
+        send(mine.at[s, pl.ds(cap, cap)], y_in.at[s], py_s.at[s], py_r.at[s], y_peer)
+
+    def combine(s):
+        arrived(y_in.at[s], py_r.at[s])
+        own_spread, own_weight = spread(s, expert)
+        far_spread, far_weight = spread(s, other)
+        total = own_weight * jnp.dot(
+            own_spread, mine[s, pl.ds(0, cap), :], preferred_element_type=f32
+        ) + far_weight * jnp.dot(far_spread, y_in[s], preferred_element_type=f32)
+
+        @pl.when(s == 0)
+        def _():
+            acc[...] = total
+
+        @pl.when(s > 0)
+        def _():
+            z_out[s] = total.astype(bf16)
+            send(z_out.at[s], z_in.at[s], pz_s.at[s], pz_r.at[s], z_ahead(s))
+
+    steps = ((choose, 0), (to_core, 1), (to_x, 0), (ffn, 2), (sum_core, 3), (sum_x, 4), (combine, 5))
+
+    def tick(t, carry):
+        for step, lag in steps:
+            @pl.when((t >= lag) & (t < depth + lag))
+            def _():
+                step(t - lag)
+        return carry
+
+    lax.fori_loop(0, depth + steps[-1][1], tick, 0)
+
+    total = acc[...]
+    for s in range(1, depth):
+        arrived(z_in.at[s], pz_r.at[s])
+        total = total + z_in[s].astype(f32)
+    out[...] = total.astype(bf16)
+    for s in range(depth):
+        if s:
+            arrived(meta_buf.at[s], zm_s.at[s])
+            arrived(tok_buf.at[s], zt_s.at[s])
+            arrived(z_out.at[s], pz_s.at[s])
+        arrived(y_out.at[s], y_s.at[s])
+        arrived(x_in.at[s], x_s.at[s])
+        arrived(c_in.at[s], c_s.at[s])
+        arrived(c_in.at[s], pc_s.at[s])
+        arrived(x_out.at[s], px_s.at[s])
+        arrived(y_in.at[s], py_s.at[s])
+
+
+def gathered_plan(tokens, expert_ids, gate_codes, w_gate, w_up, w_down, capacity, expert_count):
+    rows, top = expert_ids.shape
+    width = tokens.shape[1]
+    part_width = w_gate.shape[2]
+    depth = lax.axis_size("expert") // 2
+    f32, bf16 = jnp.float32, jnp.bfloat16
+    onehot = expert_ids[:, :, None] == jnp.arange(expert_count, dtype=jnp.int32)
+    named = jnp.sum(onehot.astype(f32), axis=1)
+    weights = jnp.sum(
+        jnp.where(onehot, (gate_codes.astype(f32) / 65536.0)[:, :, None], 0.0), axis=1
+    )
+    before = jnp.arange(rows)[:, None] >= jnp.arange(rows)[None, :]
+    counts = jnp.sum(jnp.where(before[:, :, None], named[None, :, :], 0.0), axis=1)
+    ranks = jnp.where(named > 0, counts - 1.0, -1.0)
+    table = jnp.concatenate([ranks, weights], axis=1)
+    flat = jnp.pad(table, ((0, 0), (0, LANES - 2 * expert_count)))
+    turned = jnp.pad(table.T, ((0, 0), (0, LANES - rows)))
+    meta = jnp.concatenate([flat, turned], axis=0)
+    group = 2 * capacity
+    vm = pltpu.VMEM
+    pairs = [pltpu.SemaphoreType.DMA((depth,))] * 18
+    return pl.pallas_call(
+        functools.partial(fused, depth, expert_count, capacity),
+        out_shape=jax.ShapeDtypeStruct((rows, width), bf16),
+        in_specs=[pl.BlockSpec(memory_space=pltpu.VMEM)] * 2
+        + [pl.BlockSpec(memory_space=pl.ANY)] * 3,
+        out_specs=pl.BlockSpec(memory_space=pltpu.VMEM),
+        scratch_shapes=[
+            vm((depth, rows, width), bf16),
+            vm((depth,) + meta.shape, f32),
+            vm((depth, capacity, width), bf16),
+            vm((depth, 4 * group, width), bf16),
+            vm(w_gate.shape[1:], bf16),
+            vm(w_up.shape[1:], bf16),
+            vm(w_down.shape[1:], bf16),
+            vm((4 * group, part_width), bf16),
+            vm((depth, 4 * group, width), bf16),
+            vm((depth, 2 * group, width), bf16),
+            vm((depth, group, width), bf16),
+            vm((depth, group, width), bf16),
+            vm((depth, group, width), bf16),
+            vm((depth, capacity, width), bf16),
+            vm((depth, rows, width), bf16),
+            vm((depth, rows, width), bf16),
+            vm((rows, width), f32),
+            pltpu.SemaphoreType.DMA((3,)),
+        ] + pairs,
+        compiler_params=pltpu.CompilerParams(
+            collective_id=0, has_side_effects=True, vmem_limit_bytes=63 << 20
+        ),
+    )(tokens, meta, w_gate, w_up, w_down)
+
+
+def slot_plan(tokens, expert_ids, gate_codes, w_gate, w_up, w_down):
     tok_rows, top_count = expert_ids.shape
     width = tokens.shape[1]
     expert_count = lax.axis_size("expert") * w_gate.shape[0]
@@ -43,6 +274,17 @@
     gates = gate_codes.astype(jnp.float32) / 65536.0
     weighted = per_choice.reshape(tok_rows, top_count, width) * gates[:, :, None]
     return jnp.sum(weighted, axis=1).astype(jnp.bfloat16)
+
+
+def on_device(tokens, expert_ids, gate_codes, w_gate, w_up, w_down):
+    rows, top = expert_ids.shape
+    expert_count = lax.axis_size("expert") * w_gate.shape[0]
+    capacity = 3 * rows * top // (2 * expert_count)
+    args = (tokens, expert_ids, gate_codes, w_gate, w_up, w_down)
+    paired = w_gate.shape[0] == 1 and lax.axis_size("replica") == 2 * CORES
+    if paired and 2 * capacity > rows:
+        return gathered_plan(*args, capacity, expert_count)
+    return slot_plan(*args)
 
 
 def solution(mesh):

time: 324 us -> 160 us (0.49)
  waiting for transfers between devices: 188 us -> 0 us
  Pallas kernels: 0 us -> 141 us
  blocking collectives: 59.4 us -> 0 us
  matrix products: 38.7 us -> 0 us
  between operations: 13.5 us -> 0.03 us
  starting transfers between devices: 5.56 us -> 0 us
    pallas_call x0 -> x1, Pallas kernels: none -> 141 us  [gathered_plan(): pl.pallas_call(functools.partial(fused, depth, expert_count, capacity), o...]
    reduce_scatter x1 -> x0, waiting for transfers between devices: 75.6 us -> none  [on_device(): lax.psum_scatter(jnp.dot(hidden, w_down[0], preferred_element_type=jnp.fl...]
    all_gather x1 -> x0, waiting for transfers between devices: 60.9 us -> none  [on_device(): gathered = lax.all_gather(arrived, 'replica', axis=0, tiled=True)]
    all_to_all x1 -> x0, blocking collectives: 59.4 us -> none  [on_device(): lax.all_to_all(outgoing, 'expert', split_axis=0, concat_axis=0, tiled=True)]
    all_to_all x1 -> x0, waiting for transfers between devices: 51.6 us -> none  [on_device(): lax.all_to_all(summed, 'expert', split_axis=0, concat_axis=0, tiled=True)]
    dot_general x4 -> x0, matrix products: 38.7 us -> none  [the longest x1 23.8 us: on_device(): jnp.dot(hidden, w_down[0], preferred_element_type=jnp.float32)]
    all_to_all x1 -> x0, starting transfers between devices: 5.52 us -> none  [on_device(): lax.all_to_all(summed, 'expert', split_axis=0, concat_axis=0, tiled=True)]
    unnamed x6 -> x4, local copies, waits for them, and re-layouts: 13.3 us -> 14.9 us
  transfers between devices with their start and end apart: 3 -> 0, of which waited for: 3 -> 0; matrix products, arithmetic and copies ran while one was open for 0% -> 0% of each run, Pallas kernels for 0% -> 0%
where the time goes in v1:
time: 160 us; the launch traced here: 158 us
  Pallas kernels  141 us (88%)
  local copies, waits for them, and re-layouts  14.9 us (9%)
  other arithmetic  2.18 us (1%)
    pallas_call x1, Pallas kernels, gathered_plan(): pl.pallas_call(functools.partial(fused, depth, expert_count, capacity), o...  141 us
    unnamed x4, local copies, waits for them, and re-layouts  14.9 us

profile of v1, /device:TPU:0, one launch (start us, length us, event | category | flops | bytes accessed | tf_op | source)
XLA Modules:
  0.0 157.8 jit_solution(11470523636820918502)
XLA Ops:
  0.0 0.7 convert_multiply_fusion
  0.7 0.7 convert_reduce_fusion
  1.4 0.1 select_reduce_fusion
  1.5 0.1 copy.13
  1.6 0.1 copy.17
  1.7 0.6 select_maximum_fusion.meta
  2.3 6.5 %copy.15.w_gate = bf16[1,2880,720]{2,1,0:T(8,128)(2,1)} copy(bf16[1,2880,720]{1,2,0:T(8,128)(2,1)} %param.9) | data formatting | bytes 8294400 | tf_op args[3]
  8.8 6.5 %copy.16.w_up = bf16[1,2880,720]{2,1,0:T(8,128)(2,1)} copy(bf16[1,2880,720]{1,2,0:T(8,128)(2,1)} %param.10) | data formatting | bytes 8294400 | tf_op args[4]
  15.4 140.7 %shard_map.64 = bf16[64,2880]{1,0:T(8,128)(2,1)} custom-call(bf16[64,2880]{1,0:T(8,128)(2,1)} %tokens.1, f32[80,128]{1,0:T(8,128)} %select_maximum_fusion.meta, bf16[1,2880,720]{2,1,0:T(8,128)(2,1)} %copy.15.w_gate, bf16[1,2880,720]{2,1,0:T(8,128)(2,1)} %copy.16.w_up, bf16[1,720,2880]{2,1,0:T(8,128)(2,1)} %w_down.1), custom_call_target="tpu_custom_call" | custom-call | tf_op jit(solution)/shard_map/pallas_call | solution.py:210
  156.0 1.8 %copy.19 = bf16[64,2880]{1,0:T(8,128)(2,1)} copy(bf16[64,2880]{1,0:T(8,128)(2,1)} %shard_map.64) | data formatting | bytes 737280
  (3 shorter events, 0.0 us)

commit v2 on v1

--- a/solution.py
+++ b/solution.py
@@ -24,8 +24,8 @@
     depth, experts, cap, tokens, meta, w_gate, w_up, w_down, out,
     tok_buf, meta_buf, y_out, x_buf, wg, wu, wd, hid, part, c_in, x_out, x_in,
     mine, y_in, z_out, z_in, acc, w_sem,
-    zt_s, zt_r, zm_s, zm_r, y_s, y_r, x_s, x_r, c_s, c_r,
-    pc_s, pc_r, px_s, px_r, py_s, py_r, pz_s, pz_r,
+    zt_s, zt_r, zm_s, zm_r, y_s, y_r, xa_s, xa_r, xb_s, xb_r, c_s, c_r,
+    pc_s, pc_r, pa_s, pa_r, pb_s, pb_r, py_s, py_r, pz_s, pz_r,
 ):
     rows, width = tokens.shape
     f32, bf16 = jnp.float32, jnp.bfloat16
@@ -94,14 +94,17 @@
         x_buf[s, pl.ds(0, cap), :] = jnp.dot(
             pick(s, expert), block, preferred_element_type=f32
         ).astype(bf16)
+        send(x_buf.at[s, pl.ds(0, cap)], x_buf.at[s, pl.ds(group, cap)],
+             xa_s.at[s], xa_r.at[s], x_peer)
 
     def to_x(s):
         arrived(y_out.at[s], y_r.at[s])
-        send(x_buf.at[s, pl.ds(0, group)], x_buf.at[s, pl.ds(group, group)],
-             x_s.at[s], x_r.at[s], x_peer)
+        send(x_buf.at[s, pl.ds(cap, cap)], x_buf.at[s, pl.ds(group + cap, cap)],
+             xb_s.at[s], xb_r.at[s], x_peer)
 
     def to_core(s):
-        arrived(x_in.at[s], x_r.at[s])
+        arrived(y_out.at[s], xa_r.at[s])
+        arrived(y_out.at[s], xb_r.at[s])
         send(x_buf.at[s, pl.ds(0, 2 * group)], x_buf.at[s, pl.ds(2 * group, 2 * group)],
              c_s.at[s], c_r.at[s], c_peer)
 
@@ -113,10 +116,11 @@
             for load in loads:
                 load.wait()
 
-        for low, high in spans(wg.shape[1], 256):
+        across = (((1,), (1,)), ((), ()))
+        for low, high in spans(wg.shape[0], 256):
             block = x_buf[s]
-            gate = jnp.dot(block, wg[:, low:high], preferred_element_type=f32)
-            up = jnp.dot(block, wu[:, low:high], preferred_element_type=f32)
+            gate = lax.dot_general(block, wg[low:high, :], across, preferred_element_type=f32)
+            up = lax.dot_general(block, wu[low:high, :], across, preferred_element_type=f32)
             hid[:, low:high] = activate(gate, up).astype(bf16)
         for low, high in spans(width, 512):
             part[s, :, low:high] = jnp.dot(
@@ -124,23 +128,36 @@
             ).astype(bf16)
         send(part.at[s, pl.ds(2 * group, 2 * group)], c_in.at[s], pc_s.at[s], pc_r.at[s], c_peer)
 
-    def sum_core(s):
+    def turn(i):
+        return (i + 1) % depth
+
+    def sum_core(i):
+        s = turn(i)
         arrived(c_in.at[s], pc_r.at[s])
-        x_out[s] = (
-            part[s, pl.ds(group, group), :].astype(f32) + c_in[s, pl.ds(group, group), :].astype(f32)
+        for low, ssem, rsem in ((cap, pa_s, pa_r), (0, pb_s, pb_r)):
+            x_out[s, pl.ds(low, cap), :] = (
+                part[s, pl.ds(group + low, cap), :].astype(f32)
+                + c_in[s, pl.ds(group + low, cap), :].astype(f32)
+            ).astype(bf16)
+            send(x_out.at[s, pl.ds(low, cap)], x_in.at[s, pl.ds(low, cap)],
+                 ssem.at[s], rsem.at[s], x_peer)
+
+    def add_up(s, low, rsem):
+        arrived(y_in.at[s], rsem.at[s])
+        mine[s, pl.ds(low, cap), :] = (
+            part[s, pl.ds(low, cap), :].astype(f32)
+            + c_in[s, pl.ds(low, cap), :].astype(f32)
+            + x_in[s, pl.ds(low, cap), :].astype(f32)
         ).astype(bf16)
-        send(x_out.at[s], x_in.at[s], px_s.at[s], px_r.at[s], x_peer)
-
-    def sum_x(s):
-        arrived(x_in.at[s], px_r.at[s])
-        mine[s] = (
-            part[s, pl.ds(0, group), :].astype(f32)
-            + c_in[s, pl.ds(0, group), :].astype(f32)
-            + x_in[s].astype(f32)
-        ).astype(bf16)
+
+    def sum_x(i):
+        s = turn(i)
+        add_up(s, cap, pa_r)
         send(mine.at[s, pl.ds(cap, cap)], y_in.at[s], py_s.at[s], py_r.at[s], y_peer)
-
-    def combine(s):
+        add_up(s, 0, pb_r)
+
+    def combine(i):
+        s = turn(i)
         arrived(y_in.at[s], py_r.at[s])
         own_spread, own_weight = spread(s, expert)
         far_spread, far_weight = spread(s, other)
@@ -157,7 +174,7 @@
             z_out[s] = total.astype(bf16)
             send(z_out.at[s], z_in.at[s], pz_s.at[s], pz_r.at[s], z_ahead(s))
 
-    steps = ((choose, 0), (to_core, 1), (to_x, 0), (ffn, 2), (sum_core, 3), (sum_x, 4), (combine, 5))
+    steps = ((choose, 0), (to_core, 1), (to_x, 0), (sum_core, 4), (ffn, 2), (sum_x, 5), (combine, 6))
 
     def tick(t, carry):
         for step, lag in steps:
@@ -179,17 +196,17 @@
             arrived(tok_buf.at[s], zt_s.at[s])
             arrived(z_out.at[s], pz_s.at[s])
         arrived(y_out.at[s], y_s.at[s])
-        arrived(x_in.at[s], x_s.at[s])
         arrived(c_in.at[s], c_s.at[s])
         arrived(c_in.at[s], pc_s.at[s])
-        arrived(x_out.at[s], px_s.at[s])
-        arrived(y_in.at[s], py_s.at[s])
+        for sem in (xa_s, xb_s, pa_s, pb_s, py_s):
+            arrived(y_in.at[s], sem.at[s])
 
 
 def gathered_plan(tokens, expert_ids, gate_codes, w_gate, w_up, w_down, capacity, expert_count):
     rows, top = expert_ids.shape
     width = tokens.shape[1]
-    part_width = w_gate.shape[2]
+    w_gate, w_up = jnp.swapaxes(w_gate, 1, 2), jnp.swapaxes(w_up, 1, 2)
+    part_width = w_gate.shape[1]
     depth = lax.axis_size("expert") // 2
     f32, bf16 = jnp.float32, jnp.bfloat16
     onehot = expert_ids[:, :, None] == jnp.arange(expert_count, dtype=jnp.int32)
@@ -206,7 +223,7 @@
     meta = jnp.concatenate([flat, turned], axis=0)
     group = 2 * capacity
     vm = pltpu.VMEM
-    pairs = [pltpu.SemaphoreType.DMA((depth,))] * 18
+    pairs = [pltpu.SemaphoreType.DMA((depth,))] * 22
     return pl.pallas_call(
         functools.partial(fused, depth, expert_count, capacity),
         out_shape=jax.ShapeDtypeStruct((rows, width), bf16),

time: 160 us -> 135 us (0.84)
  local copies, waits for them, and re-layouts: 14.9 us -> 1.9 us
  Pallas kernels: 141 us -> 129 us
    unnamed x4 -> x2, local copies, waits for them, and re-layouts: 14.9 us -> 1.84 us
    pallas_call x1, Pallas kernels: 141 us -> 129 us  [gathered_plan(): pl.pallas_call(functools.partial(fused, depth, expert_count, capacity), o...]
where the time goes in v2:
time: 135 us; the launch traced here: 133 us
  Pallas kernels  129 us (96%)
  other arithmetic  2.18 us (2%)
  local copies, waits for them, and re-layouts  1.9 us (1%)
    pallas_call x1, Pallas kernels, gathered_plan(): pl.pallas_call(functools.partial(fused, depth, expert_count, capacity), o...  129 us

profile of v2, /device:TPU:0, one launch (start us, length us, event | category | flops | bytes accessed | tf_op | source)
XLA Modules:
  0.0 133.1 jit_solution(11099000638137261008)
XLA Ops:
  0.0 0.7 convert_multiply_fusion
  0.7 0.7 convert_reduce_fusion
  1.4 0.1 select_reduce_fusion
  1.5 0.1 copy.11
  1.6 0.1 copy.13
  1.7 0.6 select_maximum_fusion.meta
  2.3 129.0 %shard_map.64 = bf16[64,2880]{1,0:T(8,128)(2,1)} custom-call(bf16[64,2880]{1,0:T(8,128)(2,1)} %tokens.1, f32[80,128]{1,0:T(8,128)} %select_maximum_fusion.meta, bf16[1,720,2880]{2,1,0:T(8,128)(2,1)} %bitcast.4, bf16[1,720,2880]{2,1,0:T(8,128)(2,1)} %bitcast.5, bf16[1,720,2880]{2,1,0:T(8,128)(2,1)} %w_down.1), custom_call_target="tpu_custom_call" | custom-call | tf_op jit(solution)/shard_map/pallas_call | solution.py:227
  131.3 1.8 %copy.15 = bf16[64,2880]{1,0:T(8,128)(2,1)} copy(bf16[64,2880]{1,0:T(8,128)(2,1)} %shard_map.64) | data formatting | bytes 737280
  (3 shorter events, 0.0 us)

commit v3 on v2

--- a/solution.py
+++ b/solution.py
@@ -18,6 +18,11 @@
 
 def spans(extent, step):
     return [(low, min(low + step, extent)) for low in range(0, extent, step)]
+
+
+def stage_hops(depth):
+    middle = depth // 2
+    return [0, middle] + [s for s in range(1, depth) if s != middle]
 
 
 def fused(
@@ -56,9 +61,10 @@
         pl.semaphore_signal(barrier, inc=1, device_id=peer, device_id_type=MESH)
     pl.semaphore_wait(barrier, depth + 2)
 
+    hops = stage_hops(depth)
     for s in range(1, depth):
-        send(meta, meta_buf.at[s], zm_s.at[s], zm_r.at[s], z_peer(s))
-        send(tokens, tok_buf.at[s], zt_s.at[s], zt_r.at[s], z_peer(s))
+        send(meta, meta_buf.at[s], zm_s.at[s], zm_r.at[s], z_peer(hops[s]))
+        send(tokens, tok_buf.at[s], zt_s.at[s], zt_r.at[s], z_peer(hops[s]))
     pltpu.make_async_copy(meta, meta_buf.at[0], zm_r.at[0]).start()
     pltpu.make_async_copy(tokens, tok_buf.at[0], zt_r.at[0]).start()
     loads = [
@@ -169,10 +175,11 @@
         def _():
             acc[...] = total
 
-        @pl.when(s > 0)
-        def _():
-            z_out[s] = total.astype(bf16)
-            send(z_out.at[s], z_in.at[s], pz_s.at[s], pz_r.at[s], z_ahead(s))
+        for k in range(1, depth):
+            @pl.when(s == k)
+            def _():
+                z_out[k] = total.astype(bf16)
+                send(z_out.at[k], z_in.at[k], pz_s.at[k], pz_r.at[k], z_ahead(hops[k]))
 
     steps = ((choose, 0), (to_core, 1), (to_x, 0), (sum_core, 4), (ffn, 2), (sum_x, 5), (combine, 6))
 

time: 135 us -> 136 us (level)
    pallas_call x1, Pallas kernels: 129 us -> 130 us  [gathered_plan(): pl.pallas_call(functools.partial(fused, depth, expert_count, capacity), o...]
where the time goes in v3:
time: 136 us; the launch traced here: 135 us
  Pallas kernels  130 us (96%)
  other arithmetic  2.18 us (2%)
  local copies, waits for them, and re-layouts  1.9 us (1%)
    pallas_call x1, Pallas kernels, gathered_plan(): pl.pallas_call(functools.partial(fused, depth, expert_count, capacity), o...  130 us

profile of v3, /device:TPU:0, one launch (start us, length us, event | category | flops | bytes accessed | tf_op | source)
XLA Modules:
  0.0 134.6 jit_solution(9297824338679558120)
XLA Ops:
  0.0 0.7 convert_multiply_fusion
  0.7 0.7 convert_reduce_fusion
  1.4 0.1 select_reduce_fusion
  1.5 0.1 copy.11
  1.6 0.1 copy.13
  1.7 0.6 select_maximum_fusion.meta
  2.3 130.5 %shard_map.64 = bf16[64,2880]{1,0:T(8,128)(2,1)} custom-call(bf16[64,2880]{1,0:T(8,128)(2,1)} %tokens.1, f32[80,128]{1,0:T(8,128)} %select_maximum_fusion.meta, bf16[1,720,2880]{2,1,0:T(8,128)(2,1)} %bitcast.4, bf16[1,720,2880]{2,1,0:T(8,128)(2,1)} %bitcast.5, bf16[1,720,2880]{2,1,0:T(8,128)(2,1)} %w_down.1), custom_call_target="tpu_custom_call" | custom-call | tf_op jit(solution)/shard_map/pallas_call | solution.py:234
  132.8 1.8 %copy.15 = bf16[64,2880]{1,0:T(8,128)(2,1)} copy(bf16[64,2880]{1,0:T(8,128)(2,1)} %shard_map.64) | data formatting | bytes 737280
  (3 shorter events, 0.0 us)
